TPU v7x, 256 devices: a whole 4x4x8 slice. The times are simulated.
256 devices in a mesh: mem: 16 (over z_hi, x, core), lev: 16 (over y, z_lo).
Axes of the slice: x: 4, y: 4, z: 8 (z_hi: 2, z_lo: 4; z = z_hi * 4 + z_lo), core: 2. Of those that a mesh axis runs over, the one named last changes fastest.
Arguments:
- alpha_weights: float32 [16, 32, 384, 512], P('mem', 'lev'), may hold values from -6 to 6
- perturbations: bfloat16 [16, 32, 393216], P('mem', None, 'lev'), may hold values from -6 to 6
- coef_x: float32 [384, 512], replicated, may hold values from 0.02 to 0.24
- coef_y: float32 [384, 512], replicated, may hold values from 0.02 to 0.24
- level_scale: float32 [32], replicated, may hold values from 0.3 to 1
- level_map: int32 [32], replicated, may hold values from 0 to 31, each once
- tile_widths: int32 [16], replicated, may hold values from 1 to 24576, 196608 in all
- band_widths: int32 [32], replicated, may hold values from 1 to 4, as said below
Outputs:
- increment: float32 [32, 393216], P('mem', 'lev')
Inputs may be any that keep to these rules, and one draw needn't show every extreme that they name: `level_map`: a permutation of the levels. `tile_widths`: sum to 196608; the largest equals 24576. `band_widths`: some level has a band of exactly 4.
All inputs are finite; a program needn't handle non-finite values.
Results may differ from a plain program's by a relative error of at most 0.0035.
Values may be sent and summed in bfloat16 or wider, within the bound.
No kernel may reach another device: no remote copies, remote signals or barrier semaphores. Data moves between devices by JAX's collectives and lax.ppermute only.
A program may use at most 64 MiB of HBM per device.

v0:
```python
import jax
import jax.numpy as jnp
from jax import lax
from jax.sharding import PartitionSpec as P

STEPS = 16


def diffuse_level(layer_field, scaled_x, scaled_y):

    def step_once(index_step, state):
        flux_x = scaled_x[:-1, :] * (state[1:, :] - state[:-1, :])
        flux_y = scaled_y[:, :-1] * (state[:, 1:] - state[:, :-1])
        zero_row = jnp.zeros((1, state.shape[1]), state.dtype)
        zero_col = jnp.zeros((state.shape[0], 1), state.dtype)
        change = jnp.concatenate([flux_x, zero_row], 0) - jnp.concatenate([zero_row, flux_x], 0)
        change = (
            change + jnp.concatenate([flux_y, zero_col], 1) - jnp.concatenate([zero_col, flux_y], 1)
        )
        return state + change

    return lax.fori_loop(0, STEPS, step_once, layer_field)


def vertical_matrix(band_widths):
    level_pos = jnp.arange(band_widths.shape[0])
    distance = jnp.abs(level_pos[:, None] - level_pos[None, :]).astype(jnp.float32)
    mutual = jnp.minimum(band_widths[:, None], band_widths[None, :]).astype(jnp.float32)
    return jnp.where(distance <= mutual, jnp.exp(-distance * distance / (mutual * mutual)), 0.0)


def body(
    alpha_weights, perturbations, coef_x, coef_y, level_scale, level_map, tile_widths, band_widths
):
    mem_dev, lev_dev, rows_x, rows_y = alpha_weights.shape
    levels = perturbations.shape[1]
    capacity = perturbations.shape[2]
    tile_count = lax.axis_size("lev")
    member_devices = lax.axis_size("mem")
    level_ids = jnp.arange(levels)
    slot_ids = lax.axis_index("lev") * lev_dev + jnp.arange(lev_dev)
    owned_levels = jnp.sum(
        jnp.where(slot_ids[:, None] == level_ids[None, :], level_map[None, :], 0), axis=1
    )
    level_gain = jnp.sum(
        jnp.where(owned_levels[:, None] == level_ids[None, :], level_scale[None, :], 0.0), axis=1
    )

    def smooth_slot(member_field, strength):
        return diffuse_level(member_field, coef_x * strength, coef_y * strength)

    smoothed = jax.vmap(jax.vmap(smooth_slot, (0, 0)), (0, None))(alpha_weights, level_gain)
    rounded = smoothed.astype(jnp.bfloat16).reshape(mem_dev, lev_dev, rows_x * rows_y)
    padded = jnp.pad(rounded, ((0, 0), (0, 0), (0, capacity)))
    starts = jnp.cumsum(tile_widths) - tile_widths

    def cut_tile(first_col):
        return lax.dynamic_slice_in_dim(padded, first_col, capacity, 2)

    outgoing = jax.vmap(cut_tile, out_axes=1)(starts)
    arrived = lax.all_to_all(outgoing, "lev", split_axis=1, concat_axis=1, tiled=True).reshape(
        mem_dev, levels, capacity
    )
    own_width = jnp.sum(jnp.where(jnp.arange(tile_count) == lax.axis_index("lev"), tile_widths, 0))
    valid_cols = jnp.arange(capacity) < own_width
    localizer = vertical_matrix(band_widths).astype(jnp.bfloat16)
    perm_onehot = (level_ids[:, None] == level_map[None, :]).astype(jnp.bfloat16)
    permuted = jnp.dot(localizer, perm_onehot, preferred_element_type=jnp.float32).astype(
        jnp.bfloat16
    )
    share_rows = levels // member_devices
    spread = jnp.einsum("ks,msc->mkc", permuted, arrived, preferred_element_type=jnp.float32)
    pert_rows = perturbations.astype(jnp.float32)
    summed = lax.psum(
        jnp.where(valid_cols[None, :], jnp.sum(pert_rows * spread, axis=0), 0.0), "mem"
    )
    result = lax.dynamic_slice_in_dim(summed, lax.axis_index("mem") * share_rows, share_rows, 0)
    return result


def solution(mesh):
    placed = (P("mem", "lev", None, None), P("mem", None, "lev"), P(), P(), P(), P(), P(), P())
    return jax.shard_map(
        body, mesh=mesh, in_specs=placed, out_specs=P("mem", "lev"), check_vma=False
    )
```

profile of v0, /device:TPU:8, one launch (start us, length us, event | category | flops | bytes accessed | tf_op | source)
XLA Modules:
  0.0 338.8 jit_solution(3615929898913939918)
XLA Ops:
  7.6 3.1 broadcast_multiply_fusion
  10.7 44.0 %while.11 = (s32[]{:T(128)}, f32[1,2,384,512]{3,2,1,0:T(8,128)S(1)}, f32[2,384,512]{2,1,0:T(8,128)}, f32[2,384,512]{2,1,0:T(8,128)S(1)}, s32[]{:T(128)}) while((s32[]{:T(128)}, f32[1,2,384,512]{3,2,1,0:T(8,128)S(1)}, f32[2,384,512]{2,1,0:T(8,128)}, f32[2,384,512]{2,1,0:T(8,128)S(1)}, s32[]{:T(128)}) %tuple.39), condition=%wide.region_4.5_spmd, body=%wide.region_3.4_spmd.sunk | while | flops 3142146 | bytes 25130072 | solution.py:22
  11.2 0.9 copy-done.1
  12.5 0.9 subtract_add_fusion.2
  14.0 0.9 copy-done.1
  15.2 0.9 subtract_add_fusion.2
  16.7 0.9 copy-done.1
  18.0 0.9 subtract_add_fusion.2
  20.7 0.9 subtract_add_fusion.2
  22.2 0.9 copy-done.1
  23.5 0.9 subtract_add_fusion.2
  26.2 0.9 subtract_add_fusion.2
  29.0 0.9 subtract_add_fusion.2
  30.5 0.9 copy-done.1
  31.8 0.9 subtract_add_fusion.2
  34.5 0.9 subtract_add_fusion.2
  37.3 0.9 subtract_add_fusion.2
  40.0 0.9 subtract_add_fusion.2
  42.8 0.9 subtract_add_fusion.2
  44.2 0.9 copy-done.1
  45.5 0.9 subtract_add_fusion.2
  48.3 0.9 subtract_add_fusion.2
  51.0 0.9 subtract_add_fusion.2
  52.5 0.9 copy-done.1
  53.8 0.9 subtract_add_fusion.2
  56.3 1.4 pad.9
  57.7 33.7 %while.12 = (s32[]{:T(128)}, bf16[1,2,221184]{2,1,0:T(2,128)(2,1)S(1)}, s32[16,3]{0,1:T(4,128)S(1)}, bf16[16,1,2,24576]{3,2,1,0:T(2,128)(2,1)}, s32[]{:T(128)}) while((s32[]{:T(128)}, bf16[1,2,221184]{2,1,0:T(2,128)(2,1)S(1)}, s32[16,3]{0,1:T(4,128)S(1)}, bf16[16,1,2,24576]{3,2,1,0:T(2,128)(2,1)}, s32[]{:T(128)}) %tuple.34), condition=%wide.while_cond, body=%wide.while_body.sunk | while | flops 2 | bytes 197729 | solution.py:58
  58.4 1.4 bitcast_dynamic-update-slice_fusion.2
  60.5 1.4 bitcast_dynamic-update-slice_fusion.2
  62.6 1.4 bitcast_dynamic-update-slice_fusion.2
  64.7 1.5 bitcast_dynamic-update-slice_fusion.2
  66.8 1.4 bitcast_dynamic-update-slice_fusion.2
  68.9 1.4 bitcast_dynamic-update-slice_fusion.2
  71.0 1.4 bitcast_dynamic-update-slice_fusion.2
  73.1 1.4 bitcast_dynamic-update-slice_fusion.2
  75.2 1.4 bitcast_dynamic-update-slice_fusion.2
  77.3 1.4 bitcast_dynamic-update-slice_fusion.2
  79.4 1.4 bitcast_dynamic-update-slice_fusion.2
  81.5 1.4 bitcast_dynamic-update-slice_fusion.2
  83.6 1.4 bitcast_dynamic-update-slice_fusion.2
  85.8 1.4 bitcast_dynamic-update-slice_fusion.2
  87.8 1.4 bitcast_dynamic-update-slice_fusion.2
  90.0 1.4 bitcast_dynamic-update-slice_fusion.2
  91.4 9.0 %all-to-all-start = ((bf16[1,16,2,24576]{3,2,0,1:T(2,128)(2,1)}), bf16[1,16,2,24576]{3,2,0,1:T(2,128)(2,1)S(1)}, u32[]{:S(2)}, u32[]{:S(2)}) async-start(bf16[1,16,2,24576]{3,2,0,1:T(2,128)(2,1)} %bitcast.4), calls=%async_computation | async-start | bytes 3145728 | tf_op jit(solution)/shard_map/all_to_all | solution.py:61
  101.1 35.8 %all-to-all-done = bf16[1,16,2,24576]{3,2,0,1:T(2,128)(2,1)S(1)} async-done(((bf16[1,16,2,24576]{3,2,0,1:T(2,128)(2,1)}), bf16[1,16,2,24576]{3,2,0,1:T(2,128)(2,1)S(1)}, u32[]{:S(2)}, u32[]{:S(2)}) %all-to-all-start) | async-done | bytes 1572896 | tf_op jit(solution)/shard_map/all_to_all | solution.py:61
  137.5 3.9 %fusion.2 = f32[32,24576]{1,0:T(8,128)} fusion(bf16[32,24576]{1,0:T(8,128)(2,1)S(1)} %reshape.55, bf16[1,32,24576]{2,1,0:T(8,128)(2,1)} %param.11, pred[24576]{0:T(1024)(128)(4,1)S(1)} %iota_compare_fusion, s32[32]{0:T(128)S(1)} %copy-done.4, s32[32]{0:T(128)S(1)} %copy-done.3), kind=kOutput, calls=%fused_computation.8 | convolution fusion | flops 52770816 | bytes 6316288 | tf_op jit(solution)/shard_map/ks,msc->mkc/dot_general | solution.py:72
  141.4 188.7 %all-reduce.8.cloned.1.call-done = f32[32,24576]{1,0:T(8,128)} async-done(((f32[32,24576]{1,0:T(8,128)}), f32[32,24576]{1,0:T(8,128)}) %all-reduce.8.cloned.1.call-update) | async-done | bytes 3145744 | tf_op jit(solution)/shard_map/psum | solution.py:74
  330.1 1.9 constant_dynamic-slice_fusion.1
  (114 shorter events, 36.5 us)
Async XLA Ops:
  6.5 0.9 copy-start.5
  6.5 0.7 copy-start.4
  7.6 3.1 copy-start
  10.7 1.4 copy-start.1
  13.5 1.4 copy-start.1
  16.2 1.4 copy-start.1
  19.0 1.4 copy-start.1
  21.7 1.4 copy-start.1
  24.5 1.4 copy-start.1
  27.2 1.4 copy-start.1
  30.0 1.4 copy-start.1
  32.7 1.4 copy-start.1
  35.5 1.4 copy-start.1
  38.2 1.4 copy-start.1
  41.0 1.4 copy-start.1
  43.7 1.4 copy-start.1
  46.5 1.4 copy-start.1
  49.2 1.4 copy-start.1
  52.0 1.4 copy-start.1
  54.7 0.7 copy-start.2
  91.4 45.4 %all-to-all-start = ((bf16[1,16,2,24576]{3,2,0,1:T(2,128)(2,1)}), bf16[1,16,2,24576]{3,2,0,1:T(2,128)(2,1)S(1)}, u32[]{:S(2)}, u32[]{:S(2)}) async-start(bf16[1,16,2,24576]{3,2,0,1:T(2,128)(2,1)} %bitcast.4), calls=%async_computation | async-start | bytes 3145728 | tf_op jit(solution)/shard_map/all_to_all | solution.py:61
  100.4 229.7 %all-reduce.8.cloned.1.call-start = ((), (), s32[]{:S(2)}) async-start(), calls=%async_computation.1 | async-start | bytes 6291456 | tf_op jit(solution)/shard_map/psum | solution.py:74
  101.1 36.4 %copy-start.3 = (s32[32]{0:T(128)S(1)}, s32[32]{0:T(128)}, u32[]{:S(2)}) copy-start(s32[32]{0:T(128)} %param.17) | copy-start | bytes 388
Sparse Core Ops, SparseCore 0:
  141.5 188.5 all-reduce.7
where the time goes:
time: 340 us; the launch traced here: 339 us
  waiting for transfers between devices  225 us (66%)
  local copies, waits for them, and re-layouts  53.2 us (16%)
  other arithmetic  34.1 us (10%)
  between operations  13.5 us (4%)
  starting transfers between devices  9.03 us (3%)
  matrix products  3.87 us (1%)
    psum x1, waiting for transfers between devices, body(): lax.psum(jnp.where(valid_cols[None, :], jnp.sum(pert_rows * spread, axis=...  189 us
    all_to_all x1, waiting for transfers between devices, body(): lax.all_to_all(outgoing, 'lev', split_axis=1, concat_axis=1, tiled=True)  35.8 us
    gather x48, local copies, waits for them, and re-layouts  33.6 us
    add x16, other arithmetic, step_once(): return state + change  15.1 us
    while x32, local copies, waits for them, and re-layouts  14.3 us
    all_to_all x1, starting transfers between devices, body(): lax.all_to_all(outgoing, 'lev', split_axis=1, concat_axis=1, tiled=True)  8.99 us
    mul x16, other arithmetic, step_once(): flux_y = scaled_y[:, :-1] * (state[:, 1:] - state[:, :-1])  8.01 us
  transfers between devices with their start and end apart: 2, of which 2 were waited for; matrix products, arithmetic and copies ran while one was open for 0% of the time, Pallas kernels for 0%

commit v1 on v0

--- a/solution.py
+++ b/solution.py
@@ -4,6 +4,12 @@
 from jax.sharding import PartitionSpec as P
 
 STEPS = 16
+
+
+def add_all(array, mesh_axis):
+    pieces = lax.all_gather(array, mesh_axis, axis=0, tiled=False)
+    total = pieces.sum(axis=0)
+    return total
 
 
 def diffuse_level(layer_field, scaled_x, scaled_y):
@@ -71,7 +77,7 @@
     share_rows = levels // member_devices
     spread = jnp.einsum("ks,msc->mkc", permuted, arrived, preferred_element_type=jnp.float32)
     pert_rows = perturbations.astype(jnp.float32)
-    summed = lax.psum(
+    summed = add_all(
         jnp.where(valid_cols[None, :], jnp.sum(pert_rows * spread, axis=0), 0.0), "mem"
     )
     result = lax.dynamic_slice_in_dim(summed, lax.axis_index("mem") * share_rows, share_rows, 0)

time: 340 us -> 610 us (1.79)
  waiting for transfers between devices: 225 us -> 479 us
  other arithmetic: 34.1 us -> 51.1 us
    all_gather x0 -> x1, waiting for transfers between devices: none -> 443 us  [add_all(): pieces = lax.all_gather(array, mesh_axis, axis=0, tiled=False)]
    psum x1 -> x0, waiting for transfers between devices: 189 us -> none  [body(): lax.psum(jnp.where(valid_cols[None, :], jnp.sum(pert_rows * spread, axis=...]
    reduce_sum x0 -> x1, other arithmetic: none -> 17 us  [add_all(): total = pieces.sum(axis=0)]
where the time goes in v1:
time: 610 us; the launch traced here: 608 us
  waiting for transfers between devices  479 us (79%)
  other arithmetic  51.1 us (8%)
  local copies, waits for them, and re-layouts  50.9 us (8%)
  between operations  13.5 us (2%)
  starting transfers between devices  9.03 us (1%)
    all_gather x1, waiting for transfers between devices, add_all(): pieces = lax.all_gather(array, mesh_axis, axis=0, tiled=False)  443 us
    all_to_all x1, waiting for transfers between devices, body(): lax.all_to_all(outgoing, 'lev', split_axis=1, concat_axis=1, tiled=True)  35.8 us
    gather x48, local copies, waits for them, and re-layouts  32.5 us
    reduce_sum x1, other arithmetic, add_all(): total = pieces.sum(axis=0)  17 us
    add x16, other arithmetic, step_once(): return state + change  15.1 us
    while x32, local copies, waits for them, and re-layouts  14.3 us
  transfers between devices with their start and end apart: 2, of which 2 were waited for; matrix products, arithmetic and copies ran while one was open for 0% of the time, Pallas kernels for 0%

profile of v1, /device:TPU:8, one launch (start us, length us, event | category | flops | bytes accessed | tf_op | source)
XLA Modules:
  0.0 607.8 jit_solution(9345515661546686561)
XLA Ops:
  8.5 3.1 broadcast_multiply_fusion
  11.6 44.0 %while.11 = (s32[]{:T(128)}, f32[1,2,384,512]{3,2,1,0:T(8,128)S(1)}, f32[2,384,512]{2,1,0:T(8,128)}, f32[2,384,512]{2,1,0:T(8,128)S(1)}, s32[]{:T(128)}) while((s32[]{:T(128)}, f32[1,2,384,512]{3,2,1,0:T(8,128)S(1)}, f32[2,384,512]{2,1,0:T(8,128)}, f32[2,384,512]{2,1,0:T(8,128)S(1)}, s32[]{:T(128)}) %tuple.39), condition=%wide.region_4.5_spmd, body=%wide.region_3.4_spmd.sunk | while | flops 3142146 | bytes 25130072 | solution.py:28
  12.1 0.9 copy-done.1
  13.4 0.9 subtract_add_fusion.2
  14.9 0.9 copy-done.1
  16.1 0.9 subtract_add_fusion.2
  17.6 0.9 copy-done.1
  18.9 0.9 subtract_add_fusion.2
  20.4 0.9 copy-done.1
  21.6 0.9 subtract_add_fusion.2
  23.1 0.9 copy-done.1
  24.4 0.9 subtract_add_fusion.2
  25.9 0.9 copy-done.1
  27.1 0.9 subtract_add_fusion.2
  28.6 0.9 copy-done.1
  29.9 0.9 subtract_add_fusion.2
  32.6 0.9 subtract_add_fusion.2
  35.4 0.9 subtract_add_fusion.2
  38.2 0.9 subtract_add_fusion.2
  40.9 0.9 subtract_add_fusion.2
  43.7 0.9 subtract_add_fusion.2
  46.4 0.9 subtract_add_fusion.2
  49.2 0.9 subtract_add_fusion.2
  51.9 0.9 subtract_add_fusion.2
  54.7 0.9 subtract_add_fusion.2
  56.3 1.4 pad.9
  57.7 32.5 %while.12 = (s32[]{:T(128)}, bf16[1,2,221184]{2,1,0:T(2,128)(2,1)S(1)}, s32[16,3]{0,1:T(4,128)S(1)}, bf16[16,1,2,24576]{3,2,1,0:T(2,128)(2,1)}, s32[]{:T(128)}) while((s32[]{:T(128)}, bf16[1,2,221184]{2,1,0:T(2,128)(2,1)S(1)}, s32[16,3]{0,1:T(4,128)S(1)}, bf16[16,1,2,24576]{3,2,1,0:T(2,128)(2,1)}, s32[]{:T(128)}) %tuple.34), condition=%wide.while_cond, body=%wide.while_body.sunk | while | flops 2 | bytes 197229 | solution.py:64
  58.4 1.4 bitcast_dynamic-update-slice_fusion.2
  60.4 1.4 bitcast_dynamic-update-slice_fusion.2
  62.4 1.4 bitcast_dynamic-update-slice_fusion.2
  64.5 1.4 bitcast_dynamic-update-slice_fusion.2
  66.5 1.4 bitcast_dynamic-update-slice_fusion.2
  68.5 1.4 bitcast_dynamic-update-slice_fusion.2
  70.6 1.4 bitcast_dynamic-update-slice_fusion.2
  72.6 1.4 bitcast_dynamic-update-slice_fusion.2
  74.6 1.4 bitcast_dynamic-update-slice_fusion.2
  76.7 1.4 bitcast_dynamic-update-slice_fusion.2
  78.7 1.4 bitcast_dynamic-update-slice_fusion.2
  80.7 1.4 bitcast_dynamic-update-slice_fusion.2
  82.7 1.4 bitcast_dynamic-update-slice_fusion.2
  84.8 1.4 bitcast_dynamic-update-slice_fusion.2
  86.8 1.4 bitcast_dynamic-update-slice_fusion.2
  88.8 1.4 bitcast_dynamic-update-slice_fusion.2
  90.3 9.0 %all-to-all-start = ((bf16[1,16,2,24576]{3,2,0,1:T(2,128)(2,1)}), bf16[1,16,2,24576]{3,2,0,1:T(2,128)(2,1)S(1)}, u32[]{:S(2)}, u32[]{:S(2)}) async-start(bf16[1,16,2,24576]{3,2,0,1:T(2,128)(2,1)} %bitcast.4), calls=%async_computation | async-start | bytes 3145728 | tf_op jit(solution)/shard_map/all_to_all | solution.py:67
  99.9 35.8 %all-to-all-done = bf16[1,16,2,24576]{3,2,0,1:T(2,128)(2,1)S(1)} async-done(((bf16[1,16,2,24576]{3,2,0,1:T(2,128)(2,1)}), bf16[1,16,2,24576]{3,2,0,1:T(2,128)(2,1)S(1)}, u32[]{:S(2)}, u32[]{:S(2)}) %all-to-all-start) | async-done | bytes 1572896 | tf_op jit(solution)/shard_map/all_to_all | solution.py:67
  136.3 3.8 fusion.1
  140.1 443.0 %all-gather.2.cloned.1.call-done = f32[16,32,24576]{2,1,0:T(8,128)} async-done(((f32[1,32,24576]{2,1,0:T(8,128)}), f32[16,32,24576]{2,1,0:T(8,128)}) %all-gather.2.cloned.1.call-update) | async-done | bytes 50331664 | tf_op jit(solution)/shard_map/all_gather | solution.py:10
  583.1 17.0 %reduce_sum.43 = f32[32,24576]{1,0:T(8,128)S(1)} reduce(f32[16,32,24576]{2,1,0:T(8,128)} %all-gather.2.cloned.1.call-done, f32[]{:T(128)} %constant.17.clone.1), dimensions={0}, to_apply=%region_6.7 | reduce | flops 11796480 | bytes 53477380 | tf_op jit(solution)/shard_map/reduce_sum | solution.py:11
  (115 shorter events, 36.5 us)
Async XLA Ops:
  6.5 1.7 copy-start.5
  6.5 1.5 copy-start.4
  6.5 0.7 copy-start.2
  8.4 3.1 copy-start
  11.6 1.4 copy-start.1
  14.3 1.4 copy-start.1
  17.1 1.4 copy-start.1
  19.8 1.4 copy-start.1
  22.6 1.4 copy-start.1
  25.3 1.4 copy-start.1
  28.1 1.4 copy-start.1
  30.9 1.4 copy-start.1
  33.6 1.4 copy-start.1
  36.4 1.4 copy-start.1
  39.1 1.4 copy-start.1
  41.9 1.4 copy-start.1
  44.6 1.4 copy-start.1
  47.4 1.4 copy-start.1
  50.1 1.4 copy-start.1
  52.9 1.4 copy-start.1
  90.3 45.4 %all-to-all-start = ((bf16[1,16,2,24576]{3,2,0,1:T(2,128)(2,1)}), bf16[1,16,2,24576]{3,2,0,1:T(2,128)(2,1)S(1)}, u32[]{:S(2)}, u32[]{:S(2)}) async-start(bf16[1,16,2,24576]{3,2,0,1:T(2,128)(2,1)} %bitcast.4), calls=%async_computation | async-start | bytes 3145728 | tf_op jit(solution)/shard_map/all_to_all | solution.py:67
  99.3 483.9 %all-gather.2.cloned.1.call-start = ((), (), s32[]{:S(2)}) async-start(), calls=%async_computation.1 | async-start | bytes 53477376 | tf_op jit(solution)/shard_map/all_gather | solution.py:10
  99.9 36.5 %copy-start.3 = (s32[32]{0:T(128)S(1)}, s32[32]{0:T(128)}, u32[]{:S(2)}) copy-start(s32[32]{0:T(128)} %param.17) | copy-start | bytes 388
Sparse Core Ops, SparseCore 0:
  140.3 442.8 all-gather.1
